TPU v7x, 256 devices: a whole 4x4x8 slice. The times are simulated.
256 devices in a mesh: band: 4 (over x), tile: 64 (over y, z, core).
Axes of the slice: x: 4, y: 4, z: 8, core: 2. Of those that a mesh axis runs over, the one named last changes fastest.
Arguments:
- granules: bfloat16 [1024, 16, 4096], P('tile', 'band'), may hold values from -6 to 6
- valid_rows: int32 [1024, 64], P('tile'), may hold values 0 or 1
- scene_order: int32 [1024], P('tile'), may hold values from 0 to 1023, each once
- intersections: int32 [1024, 4], P('tile'), may hold values from 0 to 63, all different within a row; in each aligned block of 16 rows (0 to 15, 16 to 31, ...) at most 2 rows name the same one
- row_resample: bfloat16 [1024, 4, 4096], P('tile'), may hold values from 0 to 1.4, as said below
- col_resample: bfloat16 [1024, 4, 4096], P('tile'), may hold values from 0 to 1.4, as said below
- w_in: bfloat16 [16, 256], replicated, may hold values from -1.5 to 1.5
- w_hidden: bfloat16 [2, 256, 256], replicated, may hold values from -0.375 to 0.375
- w_out: bfloat16 [256], replicated, may hold values from -1.5 to 1.5
Outputs:
- composite: float32 [16, 262144], P('band', 'tile')
Inputs may be any that keep to these rules, and one draw needn't show every extreme that they name: `intersections`: each scene names 4 different output tiles; the 16 scenes of one device name any one tile at most 2 times, a bound that some block reaches. `scene_order`: each order number appears once. `row_resample`: nonnegative resampling weights. `col_resample`: nonnegative resampling weights.
All inputs are finite; a program needn't handle non-finite values. No bound on the sum of `valid_rows` on one device may be relied on, other than what follows from the above.
Results may differ from a plain program's by a relative error of at most 0.0031.
Values may be sent and summed in bfloat16 or wider, within the bound.
No kernel may reach another device: no remote copies, remote signals or barrier semaphores. Data moves between devices by JAX's collectives and lax.ppermute only.
A program may use at most 128 MiB of HBM per device.

v0:
```python
import jax
import jax.numpy as jnp
from jax import lax
from jax.sharding import PartitionSpec as P

HUBER_ITERS = 4
SMOOTH = 2
prior_weight = 0.25
huber_delta = 0.5
edge_scale = 1.0
smooth_rate = 0.2


def extended_2(block, sides, width):
    for axis, dim in sides:
        count = lax.axis_size(axis)
        forward = [(i, i + 1) for i in range(count - 1)]
        backward = [(target, source) for source, target in forward]
        low = lax.ppermute(
            lax.slice_in_dim(block, block.shape[dim] - width, None, axis=dim), axis, forward
        )
        high = lax.ppermute(lax.slice_in_dim(block, 0, width, axis=dim), axis, backward)
        block = jnp.concatenate([low, block, high], axis=dim)
    return block


def scene_weights(pixels, valid_part, recency, w_in, w_hidden, w_out, side_cells):
    scenes, row_count = valid_part.shape
    valid_pix = jnp.broadcast_to(
        valid_part.astype(jnp.float32)[:, :, None], (scenes, row_count, side_cells)
    )
    valid_pix = valid_pix.reshape(scenes, row_count * side_cells)

    def one_scene(inputs):
        scene_pixels, scene_valid, scene_recency = inputs
        hidden = jax.nn.silu(
            jnp.einsum("cn,ch->nh", scene_pixels, w_in, preferred_element_type=jnp.float32)
        ).astype(jnp.bfloat16)
        for repeat in range(w_hidden.shape[0]):
            hidden = jax.nn.silu(
                jnp.dot(hidden, w_hidden[repeat], preferred_element_type=jnp.float32)
            ).astype(jnp.bfloat16)
        logits = jnp.dot(hidden, w_out, preferred_element_type=jnp.float32)
        return (jax.nn.sigmoid(-logits) * scene_valid * scene_recency).astype(jnp.bfloat16)

    return lax.map(one_scene, (pixels, valid_pix, recency))


def reproject(planes, rows_matrix, cols_matrix):
    half_done = jnp.einsum(
        "ncil,njl->ncij", planes, cols_matrix, preferred_element_type=jnp.float32
    ).astype(jnp.bfloat16)
    return jnp.einsum(
        "nij,ncjl->ncil", rows_matrix, half_done, preferred_element_type=jnp.float32
    ).astype(jnp.bfloat16)


def huber_merge(observed, weights):
    values = observed.astype(jnp.float32)
    plain = weights.astype(jnp.float32)[:, None, :]
    estimate = jnp.sum(plain * values, 0) / (jnp.sum(plain, 0) + prior_weight)
    for repeat in range(HUBER_ITERS):
        residual = values - estimate[None]
        huber_w = plain * huber_delta / jnp.maximum(jnp.abs(residual), huber_delta)
        estimate = jnp.sum(huber_w * values, 0) / (jnp.sum(huber_w, 0) + prior_weight)
    return estimate


def smooth_step(extended, first_col, total_cols):
    positions = first_col + jnp.arange(extended.shape[2] - 1)
    inside = ((positions >= 0) & (positions + 1 < total_cols)).astype(jnp.float32)
    across = extended[:, :, 1:] - extended[:, :, :-1]
    sideways = across / (1.0 + (across / edge_scale) ** 2) * inside
    centre = extended[:, :, 1:-1]
    upward_diff = centre[:, 1:, :] - centre[:, :-1, :]
    upward = upward_diff / (1.0 + (upward_diff / edge_scale) ** 2)
    zeros_row = jnp.zeros_like(upward[:, :1, :])
    vertical = jnp.concatenate([upward, zeros_row], 1) - jnp.concatenate([zeros_row, upward], 1)
    return centre + smooth_rate * (sideways[:, :, 1:] - sideways[:, :, :-1] + vertical)


def per_device(
    granules,
    valid_rows,
    scene_order,
    intersections,
    row_resample,
    col_resample,
    w_in,
    w_hidden,
    w_out,
):
    scenes, group_bands, pixel_count = granules.shape
    side_cells = valid_rows.shape[1]
    intersection_count = intersections.shape[1]
    tile_count = lax.axis_size("tile")
    band_count = lax.axis_size("band")
    recency = jnp.exp(1.4 * scene_order.astype(jnp.float32) / (scenes * tile_count) - 0.7)
    by_rows = lax.all_to_all(granules, "band", split_axis=2, concat_axis=1, tiled=True)
    row_count = side_cells // band_count
    valid_here = lax.dynamic_slice_in_dim(
        valid_rows, lax.axis_index("band") * row_count, row_count, 1
    )
    partial_weights = scene_weights(by_rows, valid_here, recency, w_in, w_hidden, w_out, side_cells)
    weights = lax.all_gather(partial_weights, "band", axis=1, tiled=True)
    plane_count = group_bands + 1
    planes = jnp.concatenate([granules, weights[:, None, :]], 1)
    entry_count = scenes * intersection_count
    capacity = (entry_count + tile_count - 1) // tile_count + 1
    buffer_rows = tile_count * capacity
    flat_dest = intersections.reshape(entry_count)
    onehot = (flat_dest[:, None] == jnp.arange(tile_count, dtype=jnp.int32)[None, :]).astype(
        jnp.int32
    )
    slot_rank = jnp.sum((jnp.cumsum(onehot, 0) - onehot) * onehot, 1)
    slot_index = flat_dest * capacity + slot_rank
    raw_planes = jnp.repeat(planes, intersection_count, axis=0)
    matrices = jnp.stack([row_resample, col_resample], 2).reshape(entry_count, 2, pixel_count)
    raw_out = (
        jnp.zeros((buffer_rows, plane_count, pixel_count), jnp.bfloat16)
        .at[slot_index]
        .set(raw_planes)
    )
    matrix_out = jnp.zeros((buffer_rows, 2, pixel_count), jnp.bfloat16).at[slot_index].set(matrices)
    raw_in, matrix_in = (
        lax.all_to_all(raw_out, "tile", split_axis=0, concat_axis=0, tiled=True),
        lax.all_to_all(matrix_out, "tile", split_axis=0, concat_axis=0, tiled=True),
    )
    matrix_in = matrix_in.reshape(buffer_rows, 2, side_cells, side_cells)
    incoming = reproject(
        raw_in.reshape(buffer_rows, plane_count, side_cells, side_cells),
        matrix_in[:, 0],
        matrix_in[:, 1],
    )
    incoming = incoming.reshape(buffer_rows, plane_count, pixel_count)
    estimate = huber_merge(incoming[:, :group_bands], incoming[:, group_bands])
    field = estimate.reshape(group_bands, side_cells, side_cells)
    first_col = lax.axis_index("tile") * side_cells
    total_cols = tile_count * side_cells
    for repeat in range(SMOOTH):
        extended = extended_2(field, (("tile", 2),), 1)
        field = smooth_step(extended, first_col - 1, total_cols)
    return field.reshape(group_bands, pixel_count)


def solution(mesh):
    return jax.shard_map(
        per_device,
        mesh=mesh,
        in_specs=(
            P("tile", "band", None),
            P("tile", None),
            P("tile"),
            P("tile", None),
            P("tile", None, None),
            P("tile", None, None),
            P(),
            P(),
            P(),
        ),
        out_specs=P("band", "tile"),
        check_vma=False,
    )
```

profile of v0, /device:TPU:8, one launch (start us, length us, event | category | flops | bytes accessed | tf_op | source)
XLA Modules:
  0.0 474.6 jit_solution(6735166915798410247)
XLA Ops:
  0.0 6.5 %copy.57 = bf16[16,4,4096]{0,1,2:T(4,128)(2,1)} copy(bf16[16,4,4096]{2,1,0:T(4,128)(2,1)} %param.11) | data formatting | bytes 1048576 | tf_op args[0]
  6.5 6.5 %reshape.136 = bf16[4,2,32768]{2,1,0:T(2,128)(2,1)} reshape(bf16[4096,4,16]{2,1,0:T(4,128)(2,1)} %bitcast.84) | data formatting | bytes 1048576
  13.0 4.3 all-to-all-start
  19.9 2.4 pad_maximum_fusion.1
  22.3 3.4 broadcast_in_dim.40
  25.8 8.2 %scatter_fusion.1 = bf16[128,2,4096]{2,1,0:T(2,128)(2,1)} fusion(bf16[128,2,4096]{2,1,0:T(2,128)(2,1)} %broadcast_in_dim.40, s32[64]{0:T(128)S(1)} %fusion.59, bf16[64,2,4096]{2,1,0:T(2,128)(2,1)S(1)} %pad_maximum_fusion.1), kind=kCustom, calls=%fused_computation.1 | custom fusion | bytes 3145984 | tf_op jit(solution)/shard_map/scatter | solution.py:124
  34.0 12.1 %all-to-all-start.2 = ((bf16[128,2,4096]{2,1,0:T(2,128)(2,1)}), bf16[128,2,4096]{2,1,0:T(2,128)(2,1)S(1)}, u32[]{:S(2)}, u32[]{:S(2)}) async-start(bf16[128,2,4096]{2,1,0:T(2,128)(2,1)} %scatter_fusion.1), calls=%async_computation.2 | async-start | bytes 4194304 | tf_op jit(solution)/shard_map/all_to_all | solution.py:127
  46.1 5.4 %reshape.137 = bf16[4096,4,16]{2,1,0:T(4,128)(2,1)} reshape(bf16[4,2,32768]{2,1,0:T(2,128)(2,1)} %all-to-all-done) | data formatting | bytes 1048576
  51.5 6.1 %copy.58 = bf16[16,4,4,1024]{3,2,1,0:T(4,128)(2,1)S(1)} copy(bf16[16,4,4,1024]{0,2,3,1:T(4,128)(2,1)} %bitcast.83) | data formatting | bytes 1048576 | tf_op jit(solution)/shard_map/all_to_all | solution.py:99
  57.8 74.0 %while.10 = (s32[]{:T(128)}, bf16[16,1024]{1,0:T(8,128)(2,1)S(1)}, bf16[16,16,1024]{2,1,0:T(8,128)(2,1)S(1)}, bf16[16,256]{1,0:T(8,128)(2,1)S(1)}, bf16[2,256,25...) while((s32[]{:T(128)}, bf16[16,1024]{1,0:T(8,128)(2,1)S(1)}, ...), condition=%wide.region_3.4_spmd, body=%wide.region_2.3_spmd.sunk | while | flops 281285632 | bytes 1384577 | solution.py:46
  59.3 1.6 fusion.80
  63.9 1.6 fusion.80
  68.6 1.6 fusion.80
  73.2 1.6 fusion.80
  76.3 1.5 multiply_convert_fusion.9
  77.8 1.6 fusion.80
  80.9 1.5 multiply_convert_fusion.9
  82.4 1.6 fusion.80
  85.5 1.5 multiply_convert_fusion.9
  87.0 1.6 fusion.80
  90.1 1.5 multiply_convert_fusion.9
  91.7 1.6 fusion.80
  94.8 1.5 multiply_convert_fusion.9
  96.3 1.6 fusion.80
  99.4 1.5 multiply_convert_fusion.9
  100.9 1.6 fusion.80
  104.0 1.5 multiply_convert_fusion.9
  105.5 1.6 fusion.80
  108.6 1.5 multiply_convert_fusion.9
  110.2 1.6 fusion.80
  113.2 1.5 multiply_convert_fusion.9
  114.8 1.6 fusion.80
  117.9 1.5 multiply_convert_fusion.9
  119.4 1.6 fusion.80
  122.5 1.5 multiply_convert_fusion.9
  124.0 1.6 fusion.80
  127.1 1.5 multiply_convert_fusion.9
  128.7 1.6 fusion.80
  131.7 12.8 %all_gather.3 = bf16[16,4096]{1,0:T(8,128)(2,1)S(1)} all-gather(bf16[16,1024]{1,0:T(8,128)(2,1)S(1)} %get-tuple-element.47), channel_id=1, replica_groups=mesh['band'=4,'tile'=64] {'band'}, dimensions={1}, use_global_device_ids=true | all-gather | bytes 163840 | tf_op jit(solution)/shard_map/all_gather | solution.py:105
  145.4 2.4 broadcast_in_dim.20.clone
  147.8 4.3 broadcast_in_dim.16
  152.1 11.9 %scatter_fusion = bf16[128,5,4096]{2,1,0:T(8,128)(2,1)} fusion(bf16[128,5,4096]{2,1,0:T(8,128)(2,1)} %broadcast_in_dim.16, s32[64]{0:T(128)S(1)} %fusion.59, bf16[64,5,4096]{2,1,0:T(8,128)(2,1)} %bitcast.82), kind=kCustom, calls=%fused_computation | custom fusion | bytes 7864576 | tf_op jit(solution)/shard_map/scatter | solution.py:122
  164.0 10.5 %all-to-all-start.1 = ((bf16[128,5,4096]{2,1,0:T(8,128)(2,1)}), bf16[128,5,4096]{2,1,0:T(8,128)(2,1)}, u32[]{:S(2)}, u32[]{:S(2)}) async-start(bf16[128,5,4096]{2,1,0:T(8,128)(2,1)} %scatter_fusion), calls=%async_computation.1 | async-start | bytes 16777216 | tf_op jit(solution)/shard_map/all_to_all | solution.py:126
  174.5 4.0 copy.65
  178.6 2.7 fusion.60
  181.3 3.9 copy.75
  185.2 3.8 copy.76
  189.0 169.8 %all-to-all-done.1 = bf16[128,5,4096]{2,1,0:T(8,128)(2,1)} async-done(((bf16[128,5,4096]{2,1,0:T(8,128)(2,1)}), bf16[128,5,4096]{2,1,0:T(8,128)(2,1)}, u32[]{:S(2)}, u32[]{:S(2)}) %all-to-all-start.1) | async-done | bytes 5242912 | tf_op jit(solution)/shard_map/all_to_all | solution.py:126
  358.8 10.6 %copy.62 = bf16[128,5,4096]{0,2,1:T(8,128)(2,1)} copy(bf16[128,5,4096]{2,1,0:T(8,128)(2,1)} %all-to-all-done.1) | data formatting | bytes 10485760 | tf_op jit(solution)/shard_map/all_to_all | solution.py:126
  369.5 15.7 %copy.67 = bf16[128,5,64,64]{3,2,1,0:T(8,128)(2,1)} copy(bf16[128,5,64,64]{0,3,2,1:T(8,128)(2,1)} %bitcast.81) | data formatting | bytes 10485760 | tf_op jit(solution)/shard_map/reshape | solution.py:131
  385.2 12.5 %convert_bitcast_fusion = bf16[128,5,64,64]{2,3,1,0:T(8,128)(2,1)} fusion(bf16[128,5,64,64]{3,2,1,0:T(8,128)(2,1)} %copy.67, bf16[128,1,64,64]{3,2,0,1:T(8,128)(2,1)} %copy.76, bf16[128,1,64,64]{3,2,0,1:T(8,128)(2,1)S(1)} %copy.75), kind=kOutput, calls=%fused_computation.29 | convolution fusion | flops 676331520 | bytes 12582912 | tf_op jit(solution)/shard_map/nij,ncjl->ncil/dot_general | solution.py:53
  397.7 18.1 %copy.70 = bf16[128,5,64,64]{0,3,2,1:T(8,128)(2,1)} copy(bf16[128,5,64,64]{2,3,1,0:T(8,128)(2,1)} %convert_bitcast_fusion) | data formatting | bytes 10485760 | tf_op jit(solution)/shard_map/convert_element_type | solution.py:55
  417.3 1.9 fusion.48
  419.3 2.3 fusion.23
  421.6 7.8 %fusion.47 = (f32[4,4096]{1,0:T(4,128)S(1)}, f32[4,4096]{1,0:T(4,128)S(1)}) fusion(f32[4,4096]{1,0:T(4,128)S(1)} %broadcast_divide_fusion, f32[128,4096]{0,1:T(8,128)S(1)} %get-tuple-element.72, bf16[128,5,4096]{0,2,1:T(8,128)(2,1)S(1)} %bitcast.77), kind=kLoop, calls=%fused_computation.53 | loop fusion | flops 16744448 | bytes 6488064 | tf_op jit(solution)/shard_map/reduce_sum | solution.py:65
  429.4 7.6 %fusion.46 = (f32[4,4096]{1,0:T(4,128)S(1)}, f32[4,4096]{1,0:T(4,128)S(1)}) fusion(f32[4,4096]{1,0:T(4,128)S(1)} %add_divide_fusion.5, f32[128,4096]{0,1:T(8,128)S(1)} %get-tuple-element.72, bf16[128,5,4096]{0,2,1:T(8,128)(2,1)S(1)} %bitcast.78), kind=kLoop, calls=%fused_computation.52 | loop fusion | flops 16744448 | bytes 6488064 | tf_op jit(solution)/shard_map/reduce_sum | solution.py:65
  437.1 7.6 %fusion.45 = (f32[4,4096]{1,0:T(4,128)S(1)}, f32[4,4096]{1,0:T(4,128)S(1)}) fusion(f32[4,4096]{1,0:T(4,128)S(1)} %add_divide_fusion.4, f32[128,4096]{0,1:T(8,128)S(1)} %get-tuple-element.72, bf16[128,5,4096]{0,2,1:T(8,128)(2,1)S(1)} %bitcast.79), kind=kLoop, calls=%fused_computation.51 | loop fusion | flops 16744448 | bytes 6488064 | tf_op jit(solution)/shard_map/reduce_sum | solution.py:65
  444.7 7.6 %fusion.44 = (f32[4,4096]{1,0:T(4,128)S(1)}, f32[4,4096]{1,0:T(4,128)S(1)}) fusion(f32[4,4096]{1,0:T(4,128)S(1)} %add_divide_fusion.3, f32[128,4096]{0,1:T(8,128)S(1)} %get-tuple-element.72, bf16[128,5,4096]{0,2,1:T(8,128)(2,1)S(1)} %bitcast.80), kind=kLoop, calls=%fused_computation.50 | loop fusion | flops 16744448 | bytes 6488064 | tf_op jit(solution)/shard_map/reduce_sum | solution.py:65
  452.6 1.9 collective-permute-start
  454.5 3.3 collective-permute-start.1
  457.8 5.1 %collective-permute-done.1 = f32[4,64,1]{2,1,0:T(8,128)S(1)} collective-permute-done((f32[4,64,1]{2,1,0:T(8,128)S(1)}, f32[4,64,1]{2,1,0:T(8,128)S(1)}, u32[]{:S(2)}, u32[]{:S(2)}) %collective-permute-start.1) | collective-permute-done | bytes 1056 | tf_op jit(solution)/shard_map/ppermute | solution.py:19
  463.3 1.9 collective-permute-start.2
  465.2 2.4 collective-permute-start.3
  467.7 5.9 %collective-permute-done.3 = f32[4,64,1]{2,1,0:T(8,128)S(1)} collective-permute-done((f32[4,64,1]{2,1,0:T(8,128)S(1)}, f32[4,64,1]{2,1,0:T(8,128)S(1)}, u32[]{:S(2)}, u32[]{:S(2)}) %collective-permute-start.3) | collective-permute-done | bytes 1056 | tf_op jit(solution)/shard_map/ppermute | solution.py:19
  (161 shorter events, 36.2 us)
Async XLA Ops:
  0.0 17.3 %copy-start.4 = (s32[16,4]{0,1:T(4,128)S(1)}, s32[16,4]{0,1:T(4,128)}, u32[]{:S(2)}) copy-start(s32[16,4]{0,1:T(4,128)} %param.14) | copy-start | bytes 772
  0.0 17.4 %copy-start.5 = (s32[16,64]{1,0:T(8,128)S(1)}, s32[16,64]{1,0:T(8,128)}, u32[]{:S(2)}) copy-start(s32[16,64]{1,0:T(8,128)} %param.12) | copy-start | bytes 12292
  0.0 18.3 %copy-start.2 = (bf16[16,4,4096]{2,1,0:T(4,128)(2,1)S(1)}, bf16[16,4,4096]{2,1,0:T(4,128)(2,1)}, u32[]{:S(2)}) copy-start(bf16[16,4,4096]{2,1,0:T(4,128)(2,1)} %param.15) | copy-start | bytes 1572868
  0.0 19.1 %copy-start.3 = (bf16[16,4,4096]{2,1,0:T(4,128)(2,1)S(1)}, bf16[16,4,4096]{2,1,0:T(4,128)(2,1)}, u32[]{:S(2)}) copy-start(bf16[16,4,4096]{2,1,0:T(4,128)(2,1)} %param.16) | copy-start | bytes 1572868
  6.5 27.5 %copy-start.8 = (s32[16]{0:T(128)S(1)}, s32[16]{0:T(128)}, u32[]{:S(2)}) copy-start(s32[16]{0:T(128)} %param.13) | copy-start | bytes 196
  13.0 21.0 %all-to-all-start = ((bf16[4,2,32768]{2,1,0:T(2,128)(2,1)}), bf16[4,2,32768]{2,1,0:T(2,128)(2,1)}, u32[]{:S(2)}, u32[]{:S(2)}) async-start(bf16[4,2,32768]{2,1,0:T(2,128)(2,1)} %reshape.136), calls=%async_computation | async-start | bytes 1048576 | tf_op jit(solution)/shard_map/all_to_all | solution.py:99
  25.8 32.0 %copy-start.6 = (bf16[2,256,256]{2,1,0:T(8,128)(2,1)S(1)}, bf16[2,256,256]{2,1,0:T(8,128)(2,1)}, u32[]{:S(2)}) copy-start(bf16[2,256,256]{2,1,0:T(8,128)(2,1)} %param.18) | copy-start | bytes 786436
  25.8 32.0 %copy-start.7 = (bf16[16,256]{1,0:T(8,128)(2,1)S(1)}, bf16[16,256]{1,0:T(8,128)(2,1)}, u32[]{:S(2)}) copy-start(bf16[16,256]{1,0:T(8,128)(2,1)} %param.17) | copy-start | bytes 24580
  25.8 32.0 %copy-start.9 = (bf16[256]{0:T(256)(128)(2,1)S(1)}, bf16[256]{0:T(256)(128)(2,1)}, u32[]{:S(2)}) copy-start(bf16[256]{0:T(256)(128)(2,1)} %param.19) | copy-start | bytes 1540
  34.0 130.0 %all-to-all-start.2 = ((bf16[128,2,4096]{2,1,0:T(2,128)(2,1)}), bf16[128,2,4096]{2,1,0:T(2,128)(2,1)S(1)}, u32[]{:S(2)}, u32[]{:S(2)}) async-start(bf16[128,2,4096]{2,1,0:T(2,128)(2,1)} %scatter_fusion.1), calls=%async_computation.2 | async-start | bytes 4194304 | tf_op jit(solution)/shard_map/all_to_all | solution.py:127
  57.7 87.1 %copy-start.1 = (bf16[16,4,4096]{2,1,0:T(4,128)(2,1)S(1)}, bf16[16,4,4096]{2,1,0:T(4,128)(2,1)}, u32[]{:S(2)}) copy-start(bf16[16,4,4096]{2,1,0:T(4,128)(2,1)} %param.11) | copy-start | bytes 1572868
  164.0 194.8 %all-to-all-start.1 = ((bf16[128,5,4096]{2,1,0:T(8,128)(2,1)}), bf16[128,5,4096]{2,1,0:T(8,128)(2,1)}, u32[]{:S(2)}, u32[]{:S(2)}) async-start(bf16[128,5,4096]{2,1,0:T(8,128)(2,1)} %scatter_fusion), calls=%async_computation.1 | async-start | bytes 16777216 | tf_op jit(solution)/shard_map/all_to_all | solution.py:126
  415.8 3.4 copy-start
  452.6 5.3 %collective-permute-start = (f32[4,64,1]{2,1,0:T(8,128)S(1)}, f32[4,64,1]{2,1,0:T(8,128)S(1)}, u32[]{:S(2)}, u32[]{:S(2)}) collective-permute-start(f32[4,64,1]{2,1,0:T(8,128)S(1)} %get-tuple-element.78), channel_id=1, source_target_pairs={{1,0},{2,1},{3,2},{4,3},{5,4},{6,5},{7,6},{8,7},{9,8},{10,9},{11,1... | collective-permute-start | bytes 3080 | tf_op jit(solution)/shard_map/ppermute | solution.py:22
  454.5 8.4 %collective-permute-start.1 = (f32[4,64,1]{2,1,0:T(8,128)S(1)}, f32[4,64,1]{2,1,0:T(8,128)S(1)}, u32[]{:S(2)}, u32[]{:S(2)}) collective-permute-start(f32[4,64,1]{2,1,0:T(8,128)S(1)} %get-tuple-element.79), channel_id=1, source_target_pairs={{0,1},{1,2},{2,3},{3,4},{4,5},{5,6},{6,7},{7,8},{8,9},{9,10},{10,1... | collective-permute-start | bytes 3080 | tf_op jit(solution)/shard_map/ppermute | solution.py:19
  463.3 4.4 collective-permute-start.2
  465.2 8.4 %collective-permute-start.3 = (f32[4,64,1]{2,1,0:T(8,128)S(1)}, f32[4,64,1]{2,1,0:T(8,128)S(1)}, u32[]{:S(2)}, u32[]{:S(2)}) collective-permute-start(f32[4,64,1]{2,1,0:T(8,128)S(1)} %get-tuple-element.77), channel_id=1, source_target_pairs={{0,1},{1,2},{2,3},{3,4},{4,5},{5,6},{6,7},{7,8},{8,9},{9,10},{10,1... | collective-permute-start | bytes 3080 | tf_op jit(solution)/shard_map/ppermute | solution.py:19
where the time goes:
time: 477 us; the launch traced here: 475 us
  waiting for transfers between devices  181 us (38%)
  local copies, waits for them, and re-layouts  129 us (27%)
  matrix products  62.6 us (13%)
  other arithmetic  51.6 us (11%)
  starting transfers between devices  36.4 us (8%)
  blocking collectives  12.8 us (3%)
    all_to_all x1, waiting for transfers between devices, per_device(): lax.all_to_all(raw_out, 'tile', split_axis=0, concat_axis=0, tiled=True)  170 us
    reduce_sum x4, other arithmetic, huber_merge(): jnp.sum(huber_w, 0) + prior_weight  30.6 us
    unnamed x26, local copies, waits for them, and re-layouts  26.2 us
    dot_general x16, matrix products, one_scene(): logits = jnp.dot(hidden, w_out, preferred_element_type=jnp.float32)  25.4 us
    dot_general x16, matrix products, one_scene(): jnp.dot(hidden, w_hidden[repeat], preferred_element_type=jnp.float32)  24.6 us
    convert_element_type x1, local copies, waits for them, and re-layouts, reproject(): return jnp.einsum('nij,ncjl->ncil', rows_matrix, half_done, preferred_ele...  18.1 us
    reshape x1, local copies, waits for them, and re-layouts, per_device(): raw_in.reshape(buffer_rows, plane_count, side_cells, side_cells)  15.7 us
    all_gather x1, blocking collectives, per_device(): weights = lax.all_gather(partial_weights, 'band', axis=1, tiled=True)  12.8 us
  transfers between devices with their start and end apart: 7, of which 3 were waited for; matrix products, arithmetic and copies ran while one was open for 29% of the time, Pallas kernels for 0%

commit v1 on v0

--- a/solution.py
+++ b/solution.py
@@ -9,6 +9,19 @@
 huber_delta = 0.5
 edge_scale = 1.0
 smooth_rate = 0.2
+
+
+def gather_around(x, axis, dim):
+    ways = lax.axis_size(axis)
+    up = [(d, (d + 1) % ways) for d in range(ways)]
+    down = [(d, (d - 1) % ways) for d in range(ways)]
+    earlier, later = ([x], [x])
+    for _ in range(ways // 2):
+        earlier.append(lax.ppermute(earlier[-1], axis, up))
+    for _ in range((ways - 1) // 2):
+        later.append(lax.ppermute(later[-1], axis, down))
+    line = jnp.concatenate([*earlier[::-1], *later[1:]], axis=dim)
+    return jnp.roll(line, (lax.axis_index(axis) - ways // 2) * x.shape[dim], axis=dim)
 
 
 def extended_2(block, sides, width):
@@ -102,7 +115,7 @@
         valid_rows, lax.axis_index("band") * row_count, row_count, 1
     )
     partial_weights = scene_weights(by_rows, valid_here, recency, w_in, w_hidden, w_out, side_cells)
-    weights = lax.all_gather(partial_weights, "band", axis=1, tiled=True)
+    weights = gather_around(partial_weights, "band", 1)
     plane_count = group_bands + 1
     planes = jnp.concatenate([granules, weights[:, None, :]], 1)
     entry_count = scenes * intersection_count

time: 477 us -> 475 us (level)
  blocking collectives: 12.8 us -> 0 us
  starting transfers between devices: 36.4 us -> 41.8 us
  waiting for transfers between devices: 181 us -> 186 us
    all_gather x1 -> x0, blocking collectives: 12.8 us -> none  [per_device(): weights = lax.all_gather(partial_weights, 'band', axis=1, tiled=True)]
    ppermute x0 -> x3, starting transfers between devices: none -> 5.34 us  [the longest x2 2.91 us: gather_around(): earlier.append(lax.ppermute(earlier[-1], axis, up))]
    ppermute x0 -> x3, waiting for transfers between devices: none -> 5 us  [the longest x2 4.99 us: gather_around(): earlier.append(lax.ppermute(earlier[-1], axis, up))]
    unnamed x26 -> x33, local copies, waits for them, and re-layouts: 26.2 us -> 26.2 us
  transfers between devices with their start and end apart: 7 -> 10, of which waited for: 3 -> 5; matrix products, arithmetic and copies ran while one was open for 29% -> 29% of each run, Pallas kernels for 0% -> 0%
where the time goes in v1:
time: 475 us; the launch traced here: 472 us
  waiting for transfers between devices  186 us (39%)
  local copies, waits for them, and re-layouts  129 us (27%)
  matrix products  62.6 us (13%)
  other arithmetic  51.6 us (11%)
  starting transfers between devices  41.8 us (9%)
    all_to_all x1, waiting for transfers between devices, per_device(): lax.all_to_all(raw_out, 'tile', split_axis=0, concat_axis=0, tiled=True)  170 us
    reduce_sum x4, other arithmetic, huber_merge(): jnp.sum(huber_w, 0) + prior_weight  30.6 us
    unnamed x33, local copies, waits for them, and re-layouts  26.2 us
    dot_general x16, matrix products, one_scene(): logits = jnp.dot(hidden, w_out, preferred_element_type=jnp.float32)  25.4 us
    dot_general x16, matrix products, one_scene(): jnp.dot(hidden, w_hidden[repeat], preferred_element_type=jnp.float32)  24.6 us
    convert_element_type x1, local copies, waits for them, and re-layouts, reproject(): return jnp.einsum('nij,ncjl->ncil', rows_matrix, half_done, preferred_ele...  18.1 us
    reshape x1, local copies, waits for them, and re-layouts, per_device(): raw_in.reshape(buffer_rows, plane_count, side_cells, side_cells)  15.7 us
    dot_general x1, matrix products, reproject(): jnp.einsum('nij,ncjl->ncil', rows_matrix, half_done, preferred_element_ty...  12.5 us
  transfers between devices with their start and end apart: 10, of which 5 were waited for; matrix products, arithmetic and copies ran while one was open for 29% of the time, Pallas kernels for 0%

profile of v1, /device:TPU:8, one launch (start us, length us, event | category | flops | bytes accessed | tf_op | source)
XLA Modules:
  0.0 472.2 jit_solution(12859525041134505195)
XLA Ops:
  0.0 6.5 %copy.56 = bf16[16,4,4096]{0,1,2:T(4,128)(2,1)} copy(bf16[16,4,4096]{2,1,0:T(4,128)(2,1)} %param.11) | data formatting | bytes 1048576 | tf_op args[0]
  6.5 6.5 %reshape.136 = bf16[4,2,32768]{2,1,0:T(2,128)(2,1)} reshape(bf16[4096,4,16]{2,1,0:T(4,128)(2,1)} %bitcast.85) | data formatting | bytes 1048576
  13.0 4.3 all-to-all-start
  19.9 2.4 pad_maximum_fusion.1
  22.3 3.4 broadcast_in_dim.40
  25.8 8.2 %scatter_fusion.1 = bf16[128,2,4096]{2,1,0:T(2,128)(2,1)} fusion(bf16[128,2,4096]{2,1,0:T(2,128)(2,1)} %broadcast_in_dim.40, s32[64]{0:T(128)S(1)} %fusion.59, bf16[64,2,4096]{2,1,0:T(2,128)(2,1)S(1)} %pad_maximum_fusion.1), kind=kCustom, calls=%fused_computation.1 | custom fusion | bytes 3145984 | tf_op jit(solution)/shard_map/scatter | solution.py:137
  34.0 12.1 %all-to-all-start.2 = ((bf16[128,2,4096]{2,1,0:T(2,128)(2,1)}), bf16[128,2,4096]{2,1,0:T(2,128)(2,1)S(1)}, u32[]{:S(2)}, u32[]{:S(2)}) async-start(bf16[128,2,4096]{2,1,0:T(2,128)(2,1)} %scatter_fusion.1), calls=%async_computation.2 | async-start | bytes 4194304 | tf_op jit(solution)/shard_map/all_to_all | solution.py:140
  46.1 5.4 %reshape.137 = bf16[4096,4,16]{2,1,0:T(4,128)(2,1)} reshape(bf16[4,2,32768]{2,1,0:T(2,128)(2,1)} %all-to-all-done) | data formatting | bytes 1048576
  51.5 6.1 %copy.57 = bf16[16,4,4,1024]{3,2,1,0:T(4,128)(2,1)S(1)} copy(bf16[16,4,4,1024]{0,2,3,1:T(4,128)(2,1)} %bitcast.84) | data formatting | bytes 1048576 | tf_op jit(solution)/shard_map/all_to_all | solution.py:112
  57.8 74.0 %while.10 = (s32[]{:T(128)}, bf16[16,1024]{1,0:T(8,128)(2,1)S(1)}, bf16[16,16,1024]{2,1,0:T(8,128)(2,1)S(1)}, bf16[16,256]{1,0:T(8,128)(2,1)S(1)}, bf16[2,256,25...) while((s32[]{:T(128)}, bf16[16,1024]{1,0:T(8,128)(2,1)S(1)}, ...), condition=%wide.region_3.4_spmd, body=%wide.region_2.3_spmd.sunk | while | flops 281285632 | bytes 1384577 | solution.py:59
  59.3 1.6 fusion.80
  63.9 1.6 fusion.80
  68.6 1.6 fusion.80
  73.2 1.6 fusion.80
  76.3 1.5 multiply_convert_fusion.9
  77.8 1.6 fusion.80
  80.9 1.5 multiply_convert_fusion.9
  82.4 1.6 fusion.80
  85.5 1.5 multiply_convert_fusion.9
  87.0 1.6 fusion.80
  90.1 1.5 multiply_convert_fusion.9
  91.7 1.6 fusion.80
  94.8 1.5 multiply_convert_fusion.9
  96.3 1.6 fusion.80
  99.4 1.5 multiply_convert_fusion.9
  100.9 1.6 fusion.80
  104.0 1.5 multiply_convert_fusion.9
  105.5 1.6 fusion.80
  108.6 1.5 multiply_convert_fusion.9
  110.2 1.6 fusion.80
  114.8 1.6 fusion.80
  119.4 1.6 fusion.80
  124.0 1.6 fusion.80
  127.1 1.5 multiply_convert_fusion.9
  128.7 1.6 fusion.80
  131.7 2.1 collective-permute-start
  133.8 3.1 collective-permute-done
  137.7 2.4 collective-permute-start.2
  140.2 1.9 collective-permute-done.1
  143.0 2.4 broadcast_in_dim.20.clone
  145.4 4.3 broadcast_in_dim.16
  149.7 11.9 %scatter_fusion = bf16[128,5,4096]{2,1,0:T(8,128)(2,1)} fusion(bf16[128,5,4096]{2,1,0:T(8,128)(2,1)} %broadcast_in_dim.16, s32[64]{0:T(128)S(1)} %fusion.59, bf16[64,5,4096]{2,1,0:T(8,128)(2,1)} %bitcast.83), kind=kCustom, calls=%fused_computation | custom fusion | bytes 7864576 | tf_op jit(solution)/shard_map/scatter | solution.py:135
  161.6 10.5 %all-to-all-start.1 = ((bf16[128,5,4096]{2,1,0:T(8,128)(2,1)}), bf16[128,5,4096]{2,1,0:T(8,128)(2,1)}, u32[]{:S(2)}, u32[]{:S(2)}) async-start(bf16[128,5,4096]{2,1,0:T(8,128)(2,1)} %scatter_fusion), calls=%async_computation.1 | async-start | bytes 16777216 | tf_op jit(solution)/shard_map/all_to_all | solution.py:139
  172.1 4.0 copy.64
  176.2 2.7 fusion.60
  178.8 3.9 copy.74
  182.8 3.8 copy.75
  186.6 169.9 %all-to-all-done.1 = bf16[128,5,4096]{2,1,0:T(8,128)(2,1)} async-done(((bf16[128,5,4096]{2,1,0:T(8,128)(2,1)}), bf16[128,5,4096]{2,1,0:T(8,128)(2,1)}, u32[]{:S(2)}, u32[]{:S(2)}) %all-to-all-start.1) | async-done | bytes 5242912 | tf_op jit(solution)/shard_map/all_to_all | solution.py:139
  356.4 10.6 %copy.61 = bf16[128,5,4096]{0,2,1:T(8,128)(2,1)} copy(bf16[128,5,4096]{2,1,0:T(8,128)(2,1)} %all-to-all-done.1) | data formatting | bytes 10485760 | tf_op jit(solution)/shard_map/all_to_all | solution.py:139
  367.1 15.7 %copy.66 = bf16[128,5,64,64]{3,2,1,0:T(8,128)(2,1)} copy(bf16[128,5,64,64]{0,3,2,1:T(8,128)(2,1)} %bitcast.82) | data formatting | bytes 10485760 | tf_op jit(solution)/shard_map/reshape | solution.py:144
  382.8 12.5 %convert_bitcast_fusion = bf16[128,5,64,64]{2,3,1,0:T(8,128)(2,1)} fusion(bf16[128,5,64,64]{3,2,1,0:T(8,128)(2,1)} %copy.66, bf16[128,1,64,64]{3,2,0,1:T(8,128)(2,1)} %copy.75, bf16[128,1,64,64]{3,2,0,1:T(8,128)(2,1)S(1)} %copy.74), kind=kOutput, calls=%fused_computation.29 | convolution fusion | flops 676331520 | bytes 12582912 | tf_op jit(solution)/shard_map/nij,ncjl->ncil/dot_general | solution.py:66
  395.3 18.1 %copy.69 = bf16[128,5,64,64]{0,3,2,1:T(8,128)(2,1)} copy(bf16[128,5,64,64]{2,3,1,0:T(8,128)(2,1)} %convert_bitcast_fusion) | data formatting | bytes 10485760 | tf_op jit(solution)/shard_map/convert_element_type | solution.py:68
  414.9 1.9 fusion.48
  416.9 2.3 fusion.23
  419.2 7.8 %fusion.47 = (f32[4,4096]{1,0:T(4,128)S(1)}, f32[4,4096]{1,0:T(4,128)S(1)}) fusion(f32[4,4096]{1,0:T(4,128)S(1)} %broadcast_divide_fusion, f32[128,4096]{0,1:T(8,128)S(1)} %get-tuple-element.72, bf16[128,5,4096]{0,2,1:T(8,128)(2,1)S(1)} %bitcast.78), kind=kLoop, calls=%fused_computation.53 | loop fusion | flops 16744448 | bytes 6488064 | tf_op jit(solution)/shard_map/reduce_sum | solution.py:78
  427.0 7.6 %fusion.46 = (f32[4,4096]{1,0:T(4,128)S(1)}, f32[4,4096]{1,0:T(4,128)S(1)}) fusion(f32[4,4096]{1,0:T(4,128)S(1)} %add_divide_fusion.5, f32[128,4096]{0,1:T(8,128)S(1)} %get-tuple-element.72, bf16[128,5,4096]{0,2,1:T(8,128)(2,1)S(1)} %bitcast.79), kind=kLoop, calls=%fused_computation.52 | loop fusion | flops 16744448 | bytes 6488064 | tf_op jit(solution)/shard_map/reduce_sum | solution.py:78
  434.7 7.6 %fusion.45 = (f32[4,4096]{1,0:T(4,128)S(1)}, f32[4,4096]{1,0:T(4,128)S(1)}) fusion(f32[4,4096]{1,0:T(4,128)S(1)} %add_divide_fusion.4, f32[128,4096]{0,1:T(8,128)S(1)} %get-tuple-element.72, bf16[128,5,4096]{0,2,1:T(8,128)(2,1)S(1)} %bitcast.80), kind=kLoop, calls=%fused_computation.51 | loop fusion | flops 16744448 | bytes 6488064 | tf_op jit(solution)/shard_map/reduce_sum | solution.py:78
  442.3 7.6 %fusion.44 = (f32[4,4096]{1,0:T(4,128)S(1)}, f32[4,4096]{1,0:T(4,128)S(1)}) fusion(f32[4,4096]{1,0:T(4,128)S(1)} %add_divide_fusion.3, f32[128,4096]{0,1:T(8,128)S(1)} %get-tuple-element.72, bf16[128,5,4096]{0,2,1:T(8,128)(2,1)S(1)} %bitcast.81), kind=kLoop, calls=%fused_computation.50 | loop fusion | flops 16744448 | bytes 6488064 | tf_op jit(solution)/shard_map/reduce_sum | solution.py:78
  450.2 1.9 collective-permute-start.3
  452.1 3.3 collective-permute-start.4
  455.4 5.1 %collective-permute-done.4 = f32[4,64,1]{2,1,0:T(8,128)S(1)} collective-permute-done((f32[4,64,1]{2,1,0:T(8,128)S(1)}, f32[4,64,1]{2,1,0:T(8,128)S(1)}, u32[]{:S(2)}, u32[]{:S(2)}) %collective-permute-start.4) | collective-permute-done | bytes 1056 | tf_op jit(solution)/shard_map/ppermute | solution.py:32
  460.9 1.9 collective-permute-start.5
  462.8 2.4 collective-permute-start.6
  465.3 5.9 %collective-permute-done.6 = f32[4,64,1]{2,1,0:T(8,128)S(1)} collective-permute-done((f32[4,64,1]{2,1,0:T(8,128)S(1)}, f32[4,64,1]{2,1,0:T(8,128)S(1)}, u32[]{:S(2)}, u32[]{:S(2)}) %collective-permute-start.6) | collective-permute-done | bytes 1056 | tf_op jit(solution)/shard_map/ppermute | solution.py:32
  (175 shorter events, 41.7 us)
Async XLA Ops:
  0.0 17.3 %copy-start.4 = (s32[16,4]{0,1:T(4,128)S(1)}, s32[16,4]{0,1:T(4,128)}, u32[]{:S(2)}) copy-start(s32[16,4]{0,1:T(4,128)} %param.14) | copy-start | bytes 772
  0.0 17.4 %copy-start.5 = (s32[16,64]{1,0:T(8,128)S(1)}, s32[16,64]{1,0:T(8,128)}, u32[]{:S(2)}) copy-start(s32[16,64]{1,0:T(8,128)} %param.12) | copy-start | bytes 12292
  0.0 18.3 %copy-start.2 = (bf16[16,4,4096]{2,1,0:T(4,128)(2,1)S(1)}, bf16[16,4,4096]{2,1,0:T(4,128)(2,1)}, u32[]{:S(2)}) copy-start(bf16[16,4,4096]{2,1,0:T(4,128)(2,1)} %param.15) | copy-start | bytes 1572868
  0.0 19.1 %copy-start.3 = (bf16[16,4,4096]{2,1,0:T(4,128)(2,1)S(1)}, bf16[16,4,4096]{2,1,0:T(4,128)(2,1)}, u32[]{:S(2)}) copy-start(bf16[16,4,4096]{2,1,0:T(4,128)(2,1)} %param.16) | copy-start | bytes 1572868
  6.5 27.5 %copy-start.8 = (s32[16]{0:T(128)S(1)}, s32[16]{0:T(128)}, u32[]{:S(2)}) copy-start(s32[16]{0:T(128)} %param.13) | copy-start | bytes 196
  13.0 21.0 %all-to-all-start = ((bf16[4,2,32768]{2,1,0:T(2,128)(2,1)}), bf16[4,2,32768]{2,1,0:T(2,128)(2,1)}, u32[]{:S(2)}, u32[]{:S(2)}) async-start(bf16[4,2,32768]{2,1,0:T(2,128)(2,1)} %reshape.136), calls=%async_computation | async-start | bytes 1048576 | tf_op jit(solution)/shard_map/all_to_all | solution.py:112
  25.8 32.0 %copy-start.6 = (bf16[2,256,256]{2,1,0:T(8,128)(2,1)S(1)}, bf16[2,256,256]{2,1,0:T(8,128)(2,1)}, u32[]{:S(2)}) copy-start(bf16[2,256,256]{2,1,0:T(8,128)(2,1)} %param.18) | copy-start | bytes 786436
  25.8 32.0 %copy-start.7 = (bf16[16,256]{1,0:T(8,128)(2,1)S(1)}, bf16[16,256]{1,0:T(8,128)(2,1)}, u32[]{:S(2)}) copy-start(bf16[16,256]{1,0:T(8,128)(2,1)} %param.17) | copy-start | bytes 24580
  25.8 32.0 %copy-start.9 = (bf16[256]{0:T(256)(128)(2,1)S(1)}, bf16[256]{0:T(256)(128)(2,1)}, u32[]{:S(2)}) copy-start(bf16[256]{0:T(256)(128)(2,1)} %param.19) | copy-start | bytes 1540
  34.0 127.6 %all-to-all-start.2 = ((bf16[128,2,4096]{2,1,0:T(2,128)(2,1)}), bf16[128,2,4096]{2,1,0:T(2,128)(2,1)S(1)}, u32[]{:S(2)}, u32[]{:S(2)}) async-start(bf16[128,2,4096]{2,1,0:T(2,128)(2,1)} %scatter_fusion.1), calls=%async_computation.2 | async-start | bytes 4194304 | tf_op jit(solution)/shard_map/all_to_all | solution.py:140
  57.7 84.7 %copy-start.1 = (bf16[16,4,4096]{2,1,0:T(4,128)(2,1)S(1)}, bf16[16,4,4096]{2,1,0:T(4,128)(2,1)}, u32[]{:S(2)}) copy-start(bf16[16,4,4096]{2,1,0:T(4,128)(2,1)} %param.11) | copy-start | bytes 1572868
  131.7 5.2 %collective-permute-start = (bf16[16,1024]{1,0:T(8,128)(2,1)S(1)}, bf16[16,1024]{1,0:T(8,128)(2,1)S(1)}, u32[]{:S(2)}, u32[]{:S(2)}) collective-permute-start(bf16[16,1024]{1,0:T(8,128)(2,1)S(1)} %get-tuple-element.47), channel_id=1, source_target_pairs={{0,64},{64,128},{128,192},{192,0},{1,65},{65,129},{129,193},{193,1... | collective-permute-start | bytes 98312 | tf_op jit(solution)/shard_map/ppermute | solution.py:20
  136.9 5.1 %collective-permute-start.1 = (bf16[16,1024]{1,0:T(8,128)(2,1)S(1)}, bf16[16,1024]{1,0:T(8,128)(2,1)S(1)}, u32[]{:S(2)}, u32[]{:S(2)}) collective-permute-start(bf16[16,1024]{1,0:T(8,128)(2,1)S(1)} %collective-permute-done), channel_id=1, source_target_pairs={{0,64},{64,128},{128,192},{192,0},{1,65},{65,129},{129,193},{193,1... | collective-permute-start | bytes 98312 | tf_op jit(solution)/shard_map/ppermute | solution.py:20
  137.7 4.3 collective-permute-start.2
  161.6 194.8 %all-to-all-start.1 = ((bf16[128,5,4096]{2,1,0:T(8,128)(2,1)}), bf16[128,5,4096]{2,1,0:T(8,128)(2,1)}, u32[]{:S(2)}, u32[]{:S(2)}) async-start(bf16[128,5,4096]{2,1,0:T(8,128)(2,1)} %scatter_fusion), calls=%async_computation.1 | async-start | bytes 16777216 | tf_op jit(solution)/shard_map/all_to_all | solution.py:139
  413.4 3.4 copy-start
  450.2 5.3 %collective-permute-start.3 = (f32[4,64,1]{2,1,0:T(8,128)S(1)}, f32[4,64,1]{2,1,0:T(8,128)S(1)}, u32[]{:S(2)}, u32[]{:S(2)}) collective-permute-start(f32[4,64,1]{2,1,0:T(8,128)S(1)} %get-tuple-element.78), channel_id=1, source_target_pairs={{1,0},{2,1},{3,2},{4,3},{5,4},{6,5},{7,6},{8,7},{9,8},{10,9},{11,1... | collective-permute-start | bytes 3080 | tf_op jit(solution)/shard_map/ppermute | solution.py:35
  452.1 8.4 %collective-permute-start.4 = (f32[4,64,1]{2,1,0:T(8,128)S(1)}, f32[4,64,1]{2,1,0:T(8,128)S(1)}, u32[]{:S(2)}, u32[]{:S(2)}) collective-permute-start(f32[4,64,1]{2,1,0:T(8,128)S(1)} %get-tuple-element.79), channel_id=1, source_target_pairs={{0,1},{1,2},{2,3},{3,4},{4,5},{5,6},{6,7},{7,8},{8,9},{9,10},{10,1... | collective-permute-start | bytes 3080 | tf_op jit(solution)/shard_map/ppermute | solution.py:32
  460.9 4.4 collective-permute-start.5
  462.8 8.4 %collective-permute-start.6 = (f32[4,64,1]{2,1,0:T(8,128)S(1)}, f32[4,64,1]{2,1,0:T(8,128)S(1)}, u32[]{:S(2)}, u32[]{:S(2)}) collective-permute-start(f32[4,64,1]{2,1,0:T(8,128)S(1)} %get-tuple-element.77), channel_id=1, source_target_pairs={{0,1},{1,2},{2,3},{3,4},{4,5},{5,6},{6,7},{7,8},{8,9},{9,10},{10,1... | collective-permute-start | bytes 3080 | tf_op jit(solution)/shard_map/ppermute | solution.py:32
